TPU v7x, 32 devices: a whole 2x2x4 slice. The times are simulated.
32 devices in a mesh: crop: 8 (over z, x), shard: 4 (over y, core).
Axes of the slice: x: 2, y: 2, z: 4, core: 2. Of those that a mesh axis runs over, the one named last changes fastest.
Arguments:
- master: float32 [14320, 128], P('shard')
- first_moment: float32 [14320, 128], P('shard'), may hold values from -5.722046e-06 to 5.722046e-06
- second_moment: float32 [14320, 128], P('shard'), may hold values from 6.8195707e-15 to 1.0911313e-13
- step: int32 [1], replicated, may hold values from 2 to 20
- plm_table: bfloat16 [21, 1280], replicated, may hold values from -6 to 6
- plm_first: bfloat16 [1280, 5248], P('shard'), may hold values from -0.15625 to 0.15625
- plm_second: bfloat16 [2560, 1280], P('shard'), may hold values from -0.25 to 0.25
- tokens: int32 [512, 32], P(('crop', 'shard')), may hold values from 0 to 20
- lengths: int32 [512], P(('crop', 'shard')), may hold values from 12 to 32
- resolved: int32 [512, 32], P(('crop', 'shard')), may hold values 0 or 1
- coords: float32 [512, 3, 32], P(('crop', 'shard')), may hold values from -15 to 15
Outputs:
- new_master: float32 [14320, 128], P('shard')
- new_first: float32 [14320, 128], P('shard')
- new_second: float32 [14320, 128], P('shard')
- weights_low: bfloat16 [14320, 128], P('shard')
- loss: float32 [], replicated
- grad_norm: float32 [], replicated
All inputs are finite; a program needn't handle non-finite values. No bound on the sum of `resolved` on one device may be relied on, other than what follows from the above.
Results may differ from a plain program's by a relative error of at most 0.012.
The roundings to bfloat16 on the way count: a program that leaves them out, or rounds other values in their place, can miss the bound.
Values may be sent and summed in bfloat16 or wider, within the bound.
No kernel may reach another device: no remote copies, remote signals or barrier semaphores. Data moves between devices by JAX's collectives and lax.ppermute only.
A program may use at most 320 MiB of HBM per device.

v0:
```python
import jax
import jax.numpy as jnp
from jax import lax
from jax.sharding import PartitionSpec as P

NODE = 256
PAIR = 128
HEADS = 8
PAIR_HEADS = 4
PLM = 1280
PLM_FF = 2560
PLM_Z = 128
NODE_FF = 1024
PAIR_FF = 512
VOCAB = 21
BINS = 65
IPA_PTS = 4
RES = 32
MICRO = 4
beta_one = 0.9
beta_two = 0.999
learn_rate = 0.02
adam_eps = 1e-10
decay_rate = 0.01
clip_norm = 0.005
point_weight = 0.01


def layout():
    return [
        ("w_in", (PLM, NODE)),
        ("w_qkv", (NODE, 3 * NODE)),
        ("w_out", (NODE, NODE)),
        ("w_lr", (NODE, 2 * PAIR)),
        ("w_n1", (NODE, NODE_FF)),
        ("w_n2", (NODE_FF, NODE)),
        ("w_bias", (PAIR, HEADS)),
        ("w_op", (PAIR, PAIR)),
        ("w_tri", (PAIR, 5 * PAIR)),
        ("w_tri_out", (PAIR, PAIR)),
        ("w_pa", (PAIR, 4 * PAIR)),
        ("w_pa_out", (PAIR, PAIR)),
        ("w_p1", (PAIR, PAIR_FF)),
        ("w_p2", (PAIR_FF, PAIR)),
        ("w_rel", (BINS, PAIR)),
        ("w_s", (NODE, 3)),
        ("w_ipa", (NODE, 3 * NODE)),
        ("w_pts", (NODE, 6 * HEADS * IPA_PTS)),
        ("w_ipa_bias", (PAIR, HEADS)),
        ("w_ipa_out", (NODE, NODE)),
        ("w_bb", (NODE, 3)),
        ("g_node", (6, NODE)),
        ("g_pair", (6, PAIR)),
    ]


def unpack(flat):
    params = {}
    offset = 0
    for weight_name, extent in layout():
        entries = extent[0] * extent[1]
        params[weight_name] = flat[offset : offset + entries].reshape(extent)
        offset += entries
    return params


def pack(params, total):
    flat = jnp.concatenate([params[weight_name].reshape(-1) for weight_name, extent in layout()])
    return jnp.pad(flat, (0, total - flat.shape[0])).reshape(-1, 128)


def product(form, left, right):
    return jnp.einsum(
        form,
        left.astype(jnp.bfloat16),
        right.astype(jnp.bfloat16),
        preferred_element_type=jnp.float32,
    )


def passthrough(values):
    return values


def layer_norm(values, gain):
    centred = values - jnp.mean(values, axis=-1, keepdims=True)
    spread = jnp.mean(centred * centred, axis=-1, keepdims=True)
    return centred * lax.rsqrt(spread + 1e-05) * gain


def softmax_last(scores):
    expo = jnp.exp(scores - jnp.max(scores, axis=-1, keepdims=True))
    return expo / jnp.sum(expo, axis=-1, keepdims=True)


def residue_weight(lengths, resolved):
    positions = jnp.arange(resolved.shape[1])
    valid = (positions[None, :] < lengths[:, None]).astype(jnp.float32)
    first = (positions == 0).astype(jnp.float32)[None, :]
    return (jnp.maximum(resolved.astype(jnp.float32), first) * valid, valid)


def crop_loss(
    params,
    table,
    plm_first,
    plm_second,
    tokens,
    lengths,
    resolved,
    coords,
    inv_count,
    multiply,
    round_fn,
):
    crops, residues = tokens.shape
    positions = jnp.arange(residues)
    weight_res, valid = residue_weight(lengths, resolved)
    key_mask = valid[:, None, :] > 0
    pmask = (valid[:, :, None] * valid[:, None, :])[..., None]
    one_hot = (tokens[:, :, None] == jnp.arange(VOCAB)[None, None, :]).astype(jnp.float32)
    features = multiply("crv,vp->crp", one_hot, table)
    uvz = jax.nn.silu(multiply("crp,pe->cre", round_fn(layer_norm(features, 1.0)), plm_first))
    base = round_fn(uvz[..., 2 * PLM_FF :])
    plm_scores = jnp.where(
        key_mask, multiply("ciz,cjz->cij", base, base) * PLM_Z ** (-0.5), -1000000000.0
    )
    mixed = multiply(
        "cij,cje->cie", round_fn(softmax_last(plm_scores)), round_fn(uvz[..., PLM_FF : 2 * PLM_FF])
    )
    plm_out = features + multiply("cie,ep->cip", round_fn(uvz[..., :PLM_FF] * mixed), plm_second)
    node = multiply("crp,pn->crn", round_fn(layer_norm(plm_out, 1.0)), params["w_in"])
    offsets = jnp.clip(positions[None, :] - positions[:, None] + (BINS - 1) // 2, 0, BINS - 1)
    rel_hot = (offsets[:, :, None] == jnp.arange(BINS)[None, None, :]).astype(jnp.float32)
    pair = jnp.broadcast_to(
        multiply("ijb,bp->ijp", rel_hot, params["w_rel"])[None], (crops, residues, residues, PAIR)
    )
    gain_node, gain_pair = (params["g_node"], params["g_pair"])
    sides = multiply("crn,nq->crq", round_fn(layer_norm(node, gain_node[0])), params["w_lr"])
    outer = sides[:, :, None, :PAIR] * sides[:, None, :, PAIR:]
    pair = pair + multiply("cijp,pq->cijq", round_fn(outer), params["w_op"])
    tri_proj = multiply("cijp,pq->cijq", round_fn(layer_norm(pair, gain_pair[0])), params["w_tri"])
    tri_left = jax.nn.sigmoid(tri_proj[..., :PAIR]) * tri_proj[..., PAIR : 2 * PAIR] * pmask
    tri_right = (
        jax.nn.sigmoid(tri_proj[..., 2 * PAIR : 3 * PAIR])
        * tri_proj[..., 3 * PAIR : 4 * PAIR]
        * pmask
    )
    tri = multiply("cikp,cjkp->cijp", round_fn(tri_left), round_fn(tri_right))
    tri_update = multiply(
        "cijp,pq->cijq", round_fn(layer_norm(tri, gain_pair[1])), params["w_tri_out"]
    )
    pair = pair + jax.nn.sigmoid(tri_proj[..., 4 * PAIR :]) * tri_update
    pair_dim = PAIR // PAIR_HEADS
    pa_proj = multiply("cijp,pq->cijq", round_fn(layer_norm(pair, gain_pair[2])), params["w_pa"])
    pa_qkv = round_fn(pa_proj[..., : 3 * PAIR])
    pa_query = pa_qkv[..., :PAIR].reshape(crops, residues, residues, PAIR_HEADS, pair_dim)
    pa_keys = pa_qkv[..., PAIR : 2 * PAIR].reshape(crops, residues, residues, PAIR_HEADS, pair_dim)
    pa_values = pa_qkv[..., 2 * PAIR :].reshape(crops, residues, residues, PAIR_HEADS, pair_dim)
    pa_scores = multiply("cijhd,cikhd->cihjk", pa_query, pa_keys) * pair_dim ** (-0.5)
    pa_scores = jnp.where(valid[:, None, None, None, :] > 0, pa_scores, -1000000000.0)
    pa_out = multiply("cihjk,cikhd->cijhd", round_fn(softmax_last(pa_scores)), pa_values).reshape(
        crops, residues, residues, PAIR
    )
    pair = pair + multiply(
        "cijp,pq->cijq",
        round_fn(jax.nn.sigmoid(pa_proj[..., 3 * PAIR :]) * pa_out),
        params["w_pa_out"],
    )
    hidden = jax.nn.gelu(
        multiply("cijp,pf->cijf", round_fn(layer_norm(pair, gain_pair[3])), params["w_p1"]),
        approximate=True,
    )
    pair = pair + multiply("cijf,fp->cijp", round_fn(hidden), params["w_p2"])
    bias = multiply("cijp,ph->chij", round_fn(layer_norm(pair, gain_pair[4])), params["w_bias"])
    head_dim = NODE // HEADS
    qkv = round_fn(
        multiply("crn,nq->crq", round_fn(layer_norm(node, gain_node[1])), params["w_qkv"])
    )
    query = qkv[..., :NODE].reshape(crops, residues, HEADS, head_dim)
    keys = qkv[..., NODE : 2 * NODE].reshape(crops, residues, HEADS, head_dim)
    values = qkv[..., 2 * NODE :].reshape(crops, residues, HEADS, head_dim)
    scores = multiply("cihd,cjhd->chij", query, keys) * head_dim ** (-0.5) + bias
    scores = jnp.where(valid[:, None, None, :] > 0, scores, -1000000000.0)
    attended = multiply("chij,cjhd->cihd", round_fn(softmax_last(scores)), values).reshape(
        crops, residues, NODE
    )
    node = node + multiply("crn,nm->crm", round_fn(attended), params["w_out"])
    hidden_node = jax.nn.gelu(
        multiply("crn,nf->crf", round_fn(layer_norm(node, gain_node[2])), params["w_n1"]),
        approximate=True,
    )
    node = node + multiply("crf,fn->crn", round_fn(hidden_node), params["w_n2"])
    start_pos = multiply("crn,nk->crk", round_fn(layer_norm(node, gain_node[3])), params["w_s"])
    single = round_fn(layer_norm(node, gain_node[4]))
    sqkv = round_fn(multiply("crn,nq->crq", single, params["w_ipa"]))
    s_query = sqkv[..., :NODE].reshape(crops, residues, HEADS, head_dim)
    s_keys = sqkv[..., NODE : 2 * NODE].reshape(crops, residues, HEADS, head_dim)
    s_values = sqkv[..., 2 * NODE :].reshape(crops, residues, HEADS, head_dim)
    points = round_fn(multiply("crn,nq->crq", single, params["w_pts"])).reshape(
        crops, residues, 2, HEADS, IPA_PTS, 3
    )
    points = points + start_pos[:, :, None, None, None, :]
    point_diff = points[:, :, None, 0] - points[:, None, :, 1]
    dist = jnp.transpose(jnp.sum(point_diff * point_diff, axis=(-1, -2)), (0, 3, 1, 2))
    ipa_bias = multiply(
        "cijp,ph->chij", round_fn(layer_norm(pair, gain_pair[5])), params["w_ipa_bias"]
    )
    ipa_scores = (
        multiply("cihd,cjhd->chij", s_query, s_keys) * head_dim ** (-0.5)
        + ipa_bias
        - point_weight * dist
    )
    ipa_scores = jnp.where(valid[:, None, None, :] > 0, ipa_scores, -1000000000.0)
    ipa_att = multiply("chij,cjhd->cihd", round_fn(softmax_last(ipa_scores)), s_values).reshape(
        crops, residues, NODE
    )
    node = node + multiply("crn,nm->crm", round_fn(ipa_att), params["w_ipa_out"])
    predicted = start_pos + multiply(
        "crn,nk->crk", round_fn(layer_norm(node, gain_node[5])), params["w_bb"]
    )
    truth = jnp.transpose(coords, (0, 2, 1))
    pred_diff = predicted[:, :, None, :] - predicted[:, None, :, :]
    true_diff = truth[:, :, None, :] - truth[:, None, :, :]
    dist_pred = jnp.sqrt(jnp.sum(pred_diff * pred_diff, axis=-1) + 1.0)
    dist_true = jnp.sqrt(jnp.sum(true_diff * true_diff, axis=-1) + 1.0)
    error = jnp.sqrt((dist_pred - dist_true) ** 2 + 1.0) - 1.0
    pair_weight = weight_res[:, :, None] * weight_res[:, None, :]
    return jnp.sum(pair_weight * error) * inv_count


def adam_update(master, first_moment, second_moment, step, grad, norm):
    clipped = grad * jnp.minimum(1.0, clip_norm / norm)
    first = beta_one * first_moment + (1.0 - beta_one) * clipped
    second = beta_two * second_moment + (1.0 - beta_two) * clipped * clipped
    step_count = step[0].astype(jnp.float32)
    first_hat = first / (1.0 - beta_one**step_count)
    second_hat = second / (1.0 - beta_two**step_count)
    updated = master - learn_rate * (
        first_hat / (jnp.sqrt(second_hat) + adam_eps) + decay_rate * master
    )
    return (updated, first, second, updated.astype(jnp.bfloat16))


def local(
    master,
    first_moment,
    second_moment,
    step,
    plm_table,
    plm_first,
    plm_second,
    tokens,
    lengths,
    resolved,
    coords,
):
    gathered, frozen_first, frozen_second = (
        lax.all_gather(master.astype(jnp.bfloat16), "shard", axis=0, tiled=True),
        lax.all_gather(plm_first, "shard", axis=0, tiled=True),
        lax.all_gather(plm_second, "shard", axis=0, tiled=True),
    )
    params = unpack(gathered.astype(jnp.float32).reshape(-1))
    weight_res, valid = residue_weight(lengths, resolved)
    local_pairs = jnp.sum(jnp.sum(weight_res, axis=1) ** 2)
    total_pairs = lax.psum(local_pairs, ("crop", "shard"))
    inv_count = 1.0 / total_pairs
    per_micro = tokens.shape[0] // MICRO
    batches = (
        tokens.reshape(MICRO, per_micro, RES),
        lengths.reshape(MICRO, per_micro),
        resolved.reshape(MICRO, per_micro, RES),
        coords.reshape(MICRO, per_micro, 3, RES),
    )

    def micro_step(carry, batch):
        micro_tokens, micro_lengths, micro_resolved, micro_coords = batch

        def loss_of(weights):
            return crop_loss(
                weights,
                plm_table,
                frozen_first,
                frozen_second,
                micro_tokens,
                micro_lengths,
                micro_resolved,
                micro_coords,
                inv_count,
                product,
                passthrough,
            )

        value, pullback = jax.vjp(loss_of, params)
        (grads,) = pullback(jnp.float32(1.0))
        return ((jax.tree.map(jnp.add, carry[0], grads), carry[1] + value), None)

    empty_grads = jax.tree.map(jnp.zeros_like, params)
    (grads, loss_part), unused = lax.scan(micro_step, (empty_grads, jnp.float32(0.0)), batches)
    grad_rows = pack(grads, gathered.size)
    own_rows = master.shape[0]
    summed, loss = lax.psum((grad_rows, loss_part), ("crop", "shard"))
    own_grad = lax.dynamic_slice_in_dim(summed, lax.axis_index("shard") * own_rows, own_rows, 0)
    norm = jnp.sqrt(jnp.sum(summed * summed))
    updated, first, second, copy_low = adam_update(
        master, first_moment, second_moment, step, own_grad, norm
    )
    return (updated, first, second, copy_low, loss, norm)


def solution(mesh):
    placed = (
        P("shard", None),
        P("shard", None),
        P("shard", None),
        P(),
        P(),
        P("shard", None),
        P("shard", None),
        P(("crop", "shard"), None),
        P(("crop", "shard")),
        P(("crop", "shard"), None),
        P(("crop", "shard"), None, None),
    )
    return jax.shard_map(
        local,
        mesh=mesh,
        in_specs=placed,
        out_specs=(
            P("shard", None),
            P("shard", None),
            P("shard", None),
            P("shard", None),
            P(),
            P(),
        ),
        check_vma=False,
    )
```

profile of v0, /device:TPU:0, one launch (start us, length us, event | category | flops | bytes accessed | tf_op | source)
XLA Modules:
  0.0 2196.8 jit_solution(18156242039349124732)
XLA Ops:
  12.1 42.6 %psum.21 = f32[]{:T(128)} all-reduce(f32[]{:T(128)} %multiply_reduce_fusion.27), channel_id=1, replica_groups=mesh['crop'=8,'shard'=4] {'crop','shard'}, use_global_device_ids=true, to_apply=%region_2.0 | all-reduce | flops 1 | bytes 8 | tf_op jit(solution)/shard_map/psum | solution.py:266
  80.9 13.3 all-gather.7.cloned.1.call-done
  94.2 88.5 %all-gather.5.cloned.1.call-done = bf16[1280,5248]{1,0:T(8,128)(2,1)} async-done(((bf16[320,5248]{1,0:T(8,128)(2,1)}), bf16[1280,5248]{1,0:T(8,128)(2,1)}) %all-gather.5.cloned.1.call-update) | async-done | bytes 13434896 | tf_op jit(solution)/shard_map/all_gather | solution.py:260
  182.7 1802.7 %while.60 = (s32[]{:T(128)}, f32[6,256]{1,0:T(8,128)}, f32[6,128]{1,0:T(8,128)}, f32[256,3]{0,1:T(4,128)}, f32[128,8]{0,1:T(8,128)}, /*index=5*/f32[1280,256]{1,...) while((s32[]{:T(128)}, f32[6,256]{1,0:T(8,128)}, ...), condition=%wide.region_91.92_spmd.clone, body=%wide.region_3.91_spmd.clone.sunk | while | flops 12452269056 | bytes 911625600 | solution.py:299
  189.1 9.2 fusion.776
  233.4 9.0 bitcast_reduce_fusion.2
  472.6 12.2 convert_reduce_fusion.6
  484.8 9.2 convolution_convert_fusion.47
  498.7 10.0 fusion.843
  508.8 8.5 convert_bitcast_fusion.6
  517.3 10.0 convert_bitcast_fusion.5
  635.5 9.2 fusion.776
  679.5 9.0 bitcast_reduce_fusion.2
  921.6 12.4 convert_reduce_fusion.6
  934.0 9.2 convolution_convert_fusion.47
  947.9 9.8 fusion.843
  966.3 10.0 convert_bitcast_fusion.5
  1085.5 9.2 fusion.776
  1129.6 9.0 bitcast_reduce_fusion.2
  1372.0 12.2 convert_reduce_fusion.6
  1384.1 9.2 convolution_convert_fusion.47
  1398.0 9.8 fusion.843
  1416.4 10.0 convert_bitcast_fusion.5
  1535.6 9.2 fusion.776
  1579.9 9.0 bitcast_reduce_fusion.2
  1822.0 12.2 convert_reduce_fusion.6
  1834.3 9.2 convolution_convert_fusion.47
  1848.1 10.0 fusion.843
  1858.2 8.5 convert_bitcast_fusion.6
  1866.8 10.0 convert_bitcast_fusion.5
  2009.4 41.7 %psum.23 = f32[]{:T(128)} all-reduce(f32[]{:T(128)} %get-tuple-element.2691), channel_id=1, replica_groups=mesh['crop'=8,'shard'=4] {'crop','shard'}, use_global_device_ids=true, to_apply=%region_94.95 | all-reduce | flops 1 | bytes 8 | tf_op jit(solution)/shard_map/psum | solution.py:302
  2051.2 125.9 %all-reduce.35.cloned.1.call-done = f32[14320,128]{1,0:T(8,128)} async-done(((f32[14320,128]{1,0:T(8,128)}), f32[14320,128]{1,0:T(8,128)}) %all-reduce.35.cloned.1.call-update) | async-done | bytes 7331856 | tf_op jit(solution)/shard_map/psum | solution.py:302
  (3271 shorter events, 1586.0 us)
Async XLA Ops:
  7.2 48.5 %all-gather.9.cloned.1.call-start = ((), (), s32[]{:S(2)}) async-start(), calls=%async_computation.3 | async-start | bytes 4587520 | tf_op jit(solution)/shard_map/all_gather | solution.py:259
  9.8 84.4 %all-gather.7.cloned.1.call-start = ((), (), s32[]{:S(2)}) async-start(), calls=%async_computation.1 | async-start | bytes 8192000 | tf_op jit(solution)/shard_map/all_gather | solution.py:261
  10.5 172.2 %all-gather.5.cloned.1.call-start = ((), (), s32[]{:S(2)}) async-start(), calls=%async_computation | async-start | bytes 16793600 | tf_op jit(solution)/shard_map/all_gather | solution.py:260
  11.3 2165.8 %all-reduce.35.cloned.1.call-start = ((), (), s32[]{:S(2)}) async-start(), calls=%async_computation.2 | async-start | bytes 14663680 | tf_op jit(solution)/shard_map/psum | solution.py:302
  75.7 107.1 %slice-start.7 = ((bf16[14320,128]{1,0:T(8,128)(2,1)}), bf16[65,128]{1,0:T(8,128)(2,1)S(1)}, s32[]{:S(2)}) async-start(bf16[14320,128]{1,0:T(8,128)(2,1)} %reshape.1091), calls=%async_computation.11 | async-start | bytes 36864 | tf_op jit(solution)/shard_map/slice | solution.py:62
  75.7 107.1 %copy-start.181 = (bf16[21,1280]{1,0:T(8,128)(2,1)S(1)}, bf16[21,1280]{1,0:T(8,128)(2,1)}, u32[]{:S(2)}) copy-start(bf16[21,1280]{1,0:T(8,128)(2,1)} %param.17) | copy-start | bytes 161284
  182.8 120.4 %copy-start.87 = (bf16[128,512]{1,0:T(8,128)(2,1)}, bf16[128,512]{1,0:T(8,128)(2,1)S(1)}, u32[]{:S(2)}) copy-start(bf16[128,512]{1,0:T(8,128)(2,1)S(1)} %get-tuple-element.2576) | copy-start | bytes 393220 | tf_op jit(solution)/shard_map/while
  185.5 68.2 %copy-start.243 = (f32[128]{0:T(128)}, f32[128]{0:T(128)S(1)}, u32[]{:S(2)}) copy-start(f32[128]{0:T(128)S(1)} %get-tuple-element.2274) | copy-start | bytes 1540 | tf_op jit(solution)/shard_map/while
  185.5 75.0 %copy-start.227 = (f32[128]{0:T(128)}, f32[128]{0:T(128)S(1)}, u32[]{:S(2)}) copy-start(f32[128]{0:T(128)S(1)} %get-tuple-element.2279) | copy-start | bytes 1540 | tf_op jit(solution)/shard_map/while
  185.5 117.7 %copy-start.199 = (f32[128]{0:T(128)}, f32[128]{0:T(128)S(1)}, u32[]{:S(2)}) copy-start(f32[128]{0:T(128)S(1)} %get-tuple-element.2289) | copy-start | bytes 1540 | tf_op jit(solution)/shard_map/while
  188.5 65.2 %copy-start.13 = (f32[32,32,128]{2,1,0:T(8,128)}, f32[32,32,128]{2,1,0:T(8,128)S(1)}, u32[]{:S(2)}) copy-start(f32[32,32,128]{2,1,0:T(8,128)S(1)} %fusion.787) | copy-start | bytes 1572868 | tf_op jit(solution)/shard_map/while
  205.8 226.6 %copy-start.24 = (f32[4,32,256]{2,1,0:T(8,128)}, f32[4,32,256]{2,1,0:T(8,128)S(1)}, u32[]{:S(2)}) copy-start(f32[4,32,256]{2,1,0:T(8,128)S(1)} %get-tuple-element.2261) | copy-start | bytes 393220 | tf_op jit(solution)/shard_map/while
  629.2 120.1 %copy-start.87 = (bf16[128,512]{1,0:T(8,128)(2,1)}, bf16[128,512]{1,0:T(8,128)(2,1)S(1)}, u32[]{:S(2)}) copy-start(bf16[128,512]{1,0:T(8,128)(2,1)S(1)} %get-tuple-element.2576) | copy-start | bytes 393220 | tf_op jit(solution)/shard_map/while
  631.9 67.9 %copy-start.243 = (f32[128]{0:T(128)}, f32[128]{0:T(128)S(1)}, u32[]{:S(2)}) copy-start(f32[128]{0:T(128)S(1)} %get-tuple-element.2274) | copy-start | bytes 1540 | tf_op jit(solution)/shard_map/while
  631.9 74.7 %copy-start.227 = (f32[128]{0:T(128)}, f32[128]{0:T(128)S(1)}, u32[]{:S(2)}) copy-start(f32[128]{0:T(128)S(1)} %get-tuple-element.2279) | copy-start | bytes 1540 | tf_op jit(solution)/shard_map/while
  631.9 117.4 %copy-start.199 = (f32[128]{0:T(128)}, f32[128]{0:T(128)S(1)}, u32[]{:S(2)}) copy-start(f32[128]{0:T(128)S(1)} %get-tuple-element.2289) | copy-start | bytes 1540 | tf_op jit(solution)/shard_map/while
  634.9 64.9 %copy-start.13 = (f32[32,32,128]{2,1,0:T(8,128)}, f32[32,32,128]{2,1,0:T(8,128)S(1)}, u32[]{:S(2)}) copy-start(f32[32,32,128]{2,1,0:T(8,128)S(1)} %fusion.787) | copy-start | bytes 1572868 | tf_op jit(solution)/shard_map/while
  652.2 227.2 %copy-start.24 = (f32[4,32,256]{2,1,0:T(8,128)}, f32[4,32,256]{2,1,0:T(8,128)S(1)}, u32[]{:S(2)}) copy-start(f32[4,32,256]{2,1,0:T(8,128)S(1)} %get-tuple-element.2261) | copy-start | bytes 393220 | tf_op jit(solution)/shard_map/while
  1079.2 120.5 %copy-start.87 = (bf16[128,512]{1,0:T(8,128)(2,1)}, bf16[128,512]{1,0:T(8,128)(2,1)S(1)}, u32[]{:S(2)}) copy-start(bf16[128,512]{1,0:T(8,128)(2,1)S(1)} %get-tuple-element.2576) | copy-start | bytes 393220 | tf_op jit(solution)/shard_map/while
  1081.9 67.9 %copy-start.243 = (f32[128]{0:T(128)}, f32[128]{0:T(128)S(1)}, u32[]{:S(2)}) copy-start(f32[128]{0:T(128)S(1)} %get-tuple-element.2274) | copy-start | bytes 1540 | tf_op jit(solution)/shard_map/while
  1081.9 74.8 %copy-start.227 = (f32[128]{0:T(128)}, f32[128]{0:T(128)S(1)}, u32[]{:S(2)}) copy-start(f32[128]{0:T(128)S(1)} %get-tuple-element.2279) | copy-start | bytes 1540 | tf_op jit(solution)/shard_map/while
  1081.9 117.8 %copy-start.199 = (f32[128]{0:T(128)}, f32[128]{0:T(128)S(1)}, u32[]{:S(2)}) copy-start(f32[128]{0:T(128)S(1)} %get-tuple-element.2289) | copy-start | bytes 1540 | tf_op jit(solution)/shard_map/while
  1084.9 65.0 %copy-start.13 = (f32[32,32,128]{2,1,0:T(8,128)}, f32[32,32,128]{2,1,0:T(8,128)S(1)}, u32[]{:S(2)}) copy-start(f32[32,32,128]{2,1,0:T(8,128)S(1)} %fusion.787) | copy-start | bytes 1572868 | tf_op jit(solution)/shard_map/while
  1102.2 227.4 %copy-start.24 = (f32[4,32,256]{2,1,0:T(8,128)}, f32[4,32,256]{2,1,0:T(8,128)S(1)}, u32[]{:S(2)}) copy-start(f32[4,32,256]{2,1,0:T(8,128)S(1)} %get-tuple-element.2261) | copy-start | bytes 393220 | tf_op jit(solution)/shard_map/while
  1529.4 120.4 %copy-start.87 = (bf16[128,512]{1,0:T(8,128)(2,1)}, bf16[128,512]{1,0:T(8,128)(2,1)S(1)}, u32[]{:S(2)}) copy-start(bf16[128,512]{1,0:T(8,128)(2,1)S(1)} %get-tuple-element.2576) | copy-start | bytes 393220 | tf_op jit(solution)/shard_map/while
  1532.1 68.2 %copy-start.243 = (f32[128]{0:T(128)}, f32[128]{0:T(128)S(1)}, u32[]{:S(2)}) copy-start(f32[128]{0:T(128)S(1)} %get-tuple-element.2274) | copy-start | bytes 1540 | tf_op jit(solution)/shard_map/while
  1532.1 75.0 %copy-start.227 = (f32[128]{0:T(128)}, f32[128]{0:T(128)S(1)}, u32[]{:S(2)}) copy-start(f32[128]{0:T(128)S(1)} %get-tuple-element.2279) | copy-start | bytes 1540 | tf_op jit(solution)/shard_map/while
  1532.1 117.7 %copy-start.199 = (f32[128]{0:T(128)}, f32[128]{0:T(128)S(1)}, u32[]{:S(2)}) copy-start(f32[128]{0:T(128)S(1)} %get-tuple-element.2289) | copy-start | bytes 1540 | tf_op jit(solution)/shard_map/while
  1535.0 65.2 %copy-start.13 = (f32[32,32,128]{2,1,0:T(8,128)}, f32[32,32,128]{2,1,0:T(8,128)S(1)}, u32[]{:S(2)}) copy-start(f32[32,32,128]{2,1,0:T(8,128)S(1)} %fusion.787) | copy-start | bytes 1572868 | tf_op jit(solution)/shard_map/while
  1552.4 227.5 %copy-start.24 = (f32[4,32,256]{2,1,0:T(8,128)}, f32[4,32,256]{2,1,0:T(8,128)S(1)}, u32[]{:S(2)}) copy-start(f32[4,32,256]{2,1,0:T(8,128)S(1)} %get-tuple-element.2261) | copy-start | bytes 393220 | tf_op jit(solution)/shard_map/while
  1556.7 43.6 %copy-start.6 = (f32[4,32,32,128]{3,2,1,0:T(8,128)}, f32[4,32,32,128]{3,2,1,0:T(8,128)S(1)}, u32[]{:S(2)}) copy-start(f32[4,32,32,128]{3,2,1,0:T(8,128)S(1)} %get-tuple-element.2267) | copy-start | bytes 6291460 | tf_op jit(solution)/shard_map/while
  2051.2 131.4 %copy-start.127 = (f32[3580,128]{1,0:T(8,128)S(1)}, f32[3580,128]{1,0:T(8,128)}, u32[]{:S(2)}) copy-start(f32[3580,128]{1,0:T(8,128)} %param.13) | copy-start | bytes 5498884
  (1042 other events, 4159.7 us)
Sparse Core Ops, SparseCore 0:
  10.1 34.4 all-gather.8
  46.2 47.9 all-gather.6
  95.8 86.9 all-gather.4
  2008.8 168.2 all-reduce.34
where the time goes:
time: 2210 us; the launch traced here: 2200 us
  matrix products  784 us (35%)
  local copies, waits for them, and re-layouts  618 us (28%)
  other arithmetic  437 us (20%)
  waiting for transfers between devices  229 us (10%)
  blocking collectives  84.3 us (4%)
  loops' own time  25.5 us (1%)
    dot_general x344, matrix products, product(): jnp.einsum(form, left.astype(jnp.bfloat16), right.astype(jnp.bfloat16), p...  780 us
    psum x1, waiting for transfers between devices, local(): summed, loss = lax.psum((grad_rows, loss_part), ('crop', 'shard'))  126 us
    convert_element_type x56, local copies, waits for them, and re-layouts, product(): right.astype(jnp.bfloat16)  125 us
    convert_element_type x28, local copies, waits for them, and re-layouts, product(): left.astype(jnp.bfloat16)  89.2 us
    all_gather x1, waiting for transfers between devices, local(): lax.all_gather(plm_first, 'shard', axis=0, tiled=True)  88.5 us
    dot_general x28, local copies, waits for them, and re-layouts, product(): jnp.einsum(form, left.astype(jnp.bfloat16), right.astype(jnp.bfloat16), p...  84.9 us
    reduce_sum x28, other arithmetic, layer_norm(): return centred * lax.rsqrt(spread + 1e-05) * gain  80.5 us
    while x2096, local copies, waits for them, and re-layouts  50 us
  transfers between devices with their start and end apart: 4, of which 3 were waited for; matrix products, arithmetic and copies ran while one was open for 1% of the time, Pallas kernels for 0%

commit v1 on v0

--- a/solution.py
+++ b/solution.py
@@ -24,6 +24,18 @@
 decay_rate = 0.01
 clip_norm = 0.005
 point_weight = 0.01
+
+
+def doubled_up(x, axis, dim):
+    ways, here = (lax.axis_size(axis), lax.axis_index(axis))
+    grown, reach = (x, 1)
+    while reach < ways:
+        theirs = lax.ppermute(grown, axis, [(d, d ^ reach) for d in range(ways)])
+        mine_first = jnp.concatenate([grown, theirs], axis=dim)
+        theirs_first = jnp.concatenate([theirs, grown], axis=dim)
+        grown = jnp.where(here & reach == 0, mine_first, theirs_first)
+        reach = 2 * reach
+    return grown
 
 
 def layout():
@@ -257,7 +269,7 @@
 ):
     gathered, frozen_first, frozen_second = (
         lax.all_gather(master.astype(jnp.bfloat16), "shard", axis=0, tiled=True),
-        lax.all_gather(plm_first, "shard", axis=0, tiled=True),
+        doubled_up(plm_first, "shard", 0),
         lax.all_gather(plm_second, "shard", axis=0, tiled=True),
     )
     params = unpack(gathered.astype(jnp.float32).reshape(-1))

time: 2210 us -> 2330 us (1.054)
  blocking collectives: 84.3 us -> 269 us
  waiting for transfers between devices: 229 us -> 131 us
  other arithmetic: 437 us -> 465 us
    psum x1, blocking collectives: 42.6 us -> 228 us  [local(): total_pairs = lax.psum(local_pairs, ('crop', 'shard'))]
    all_gather x1 -> x0, waiting for transfers between devices: 88.5 us -> none  [local(): lax.all_gather(plm_first, 'shard', axis=0, tiled=True)]
    select_n x0 -> x2, other arithmetic: none -> 24.7 us  [doubled_up(): grown = jnp.where(here & reach == 0, mine_first, theirs_first)]
    while x2096 -> x2088, local copies, waits for them, and re-layouts: 50 us -> 49.4 us
  transfers between devices with their start and end apart: 4 -> 5, of which waited for: 3 -> 2; matrix products, arithmetic and copies ran while one was open for 1% -> 2% of each run, Pallas kernels for 0% -> 0%
where the time goes in v1:
time: 2330 us; the launch traced here: 2320 us
  matrix products  786 us (34%)
  local copies, waits for them, and re-layouts  617 us (26%)
  other arithmetic  465 us (20%)
  blocking collectives  269 us (12%)
  waiting for transfers between devices  131 us (6%)
  loops' own time  26 us (1%)
    dot_general x344, matrix products, product(): jnp.einsum(form, left.astype(jnp.bfloat16), right.astype(jnp.bfloat16), p...  782 us
    psum x1, blocking collectives, local(): total_pairs = lax.psum(local_pairs, ('crop', 'shard'))  228 us
    psum x1, waiting for transfers between devices, local(): summed, loss = lax.psum((grad_rows, loss_part), ('crop', 'shard'))  125 us
    convert_element_type x56, local copies, waits for them, and re-layouts, product(): right.astype(jnp.bfloat16)  125 us
    convert_element_type x28, local copies, waits for them, and re-layouts, product(): left.astype(jnp.bfloat16)  88.9 us
    dot_general x28, local copies, waits for them, and re-layouts, product(): jnp.einsum(form, left.astype(jnp.bfloat16), right.astype(jnp.bfloat16), p...  84.8 us
    reduce_sum x28, other arithmetic, layer_norm(): return centred * lax.rsqrt(spread + 1e-05) * gain  80.4 us
    while x2088, local copies, waits for them, and re-layouts  49.4 us
  transfers between devices with their start and end apart: 5, of which 2 were waited for; matrix products, arithmetic and copies ran while one was open for 2% of the time, Pallas kernels for 0%

profile of v1, /device:TPU:0, one launch (start us, length us, event | category | flops | bytes accessed | tf_op | source)
XLA Modules:
  0.0 2315.6 jit_solution(12886252837886479977)
XLA Ops:
  28.6 227.5 %psum.21 = f32[]{:T(128)} all-reduce(f32[]{:T(128)} %multiply_reduce_fusion.27), channel_id=1, replica_groups=mesh['crop'=8,'shard'=4] {'crop','shard'}, use_global_device_ids=true, to_apply=%region_2.3 | all-reduce | flops 1 | bytes 8 | tf_op jit(solution)/shard_map/psum | solution.py:278
  281.5 16.7 maximum_select_fusion
  298.2 1806.8 %while.60 = (s32[]{:T(128)}, f32[6,256]{1,0:T(8,128)}, f32[6,128]{1,0:T(8,128)}, f32[256,3]{0,1:T(4,128)}, f32[128,8]{0,1:T(8,128)}, /*index=5*/f32[1280,256]{1,...) while((s32[]{:T(128)}, f32[6,256]{1,0:T(8,128)}, ...), condition=%wide.region_91.92_spmd.clone, body=%wide.region_3.91_spmd.clone.sunk | while | flops 12452269056 | bytes 911617344 | solution.py:311
  305.5 9.2 fusion.776
  349.8 9.0 bitcast_reduce_fusion.2
  589.4 12.2 convert_reduce_fusion.6
  601.7 9.2 convolution_convert_fusion.47
  615.5 10.0 fusion.843
  625.6 8.5 convert_bitcast_fusion.6
  634.1 10.0 convert_bitcast_fusion.5
  752.9 9.2 fusion.776
  796.9 9.0 bitcast_reduce_fusion.2
  1039.4 12.4 convert_reduce_fusion.6
  1051.8 9.2 convolution_convert_fusion.47
  1065.7 9.8 fusion.843
  1075.5 8.5 convert_bitcast_fusion.6
  1084.1 10.0 convert_bitcast_fusion.5
  1203.9 9.2 fusion.776
  1247.9 9.0 bitcast_reduce_fusion.2
  1490.6 12.2 convert_reduce_fusion.6
  1502.8 9.2 convolution_convert_fusion.47
  1516.7 9.8 fusion.843
  1535.1 10.0 convert_bitcast_fusion.5
  1655.0 9.2 fusion.776
  1699.2 9.0 bitcast_reduce_fusion.2
  1941.7 12.2 convert_reduce_fusion.6
  1953.9 9.2 convolution_convert_fusion.47
  1967.7 10.0 fusion.843
  1977.9 8.5 convert_bitcast_fusion.6
  1986.4 10.0 convert_bitcast_fusion.5
  2129.0 41.8 %psum.23 = f32[]{:T(128)} all-reduce(f32[]{:T(128)} %get-tuple-element.2630), channel_id=1, replica_groups=mesh['crop'=8,'shard'=4] {'crop','shard'}, use_global_device_ids=true, to_apply=%region_94.95 | all-reduce | flops 1 | bytes 8 | tf_op jit(solution)/shard_map/psum | solution.py:314
  2170.8 125.1 %all-reduce.35.cloned.1.call-done = f32[14320,128]{1,0:T(8,128)} async-done(((f32[14320,128]{1,0:T(8,128)}), f32[14320,128]{1,0:T(8,128)}) %all-reduce.35.cloned.1.call-update) | async-done | bytes 7331856 | tf_op jit(solution)/shard_map/psum | solution.py:314
  (3266 shorter events, 1596.8 us)
Async XLA Ops:
  7.2 249.9 %all-gather.6.cloned.1.call-start = ((), (), s32[]{:S(2)}) async-start(), calls=%async_computation.2 | async-start | bytes 4587520 | tf_op jit(solution)/shard_map/all_gather | solution.py:271
  9.9 288.3 %all-gather.4.cloned.1.call-start = ((), (), s32[]{:S(2)}) async-start(), calls=%async_computation | async-start | bytes 8192000 | tf_op jit(solution)/shard_map/all_gather | solution.py:273
  10.0 6.3 collective-permute-start
  10.7 2285.3 %all-reduce.35.cloned.1.call-start = ((), (), s32[]{:S(2)}) async-start(), calls=%async_computation.1 | async-start | bytes 14663680 | tf_op jit(solution)/shard_map/psum | solution.py:314
  24.2 257.3 %collective-permute-start.1 = (bf16[640,5248]{1,0:T(8,128)(2,1)}, bf16[640,5248]{1,0:T(8,128)(2,1)}, u32[]{:S(2)}, u32[]{:S(2)}) collective-permute-start(bf16[640,5248]{1,0:T(8,128)(2,1)} %maximum_select_fusion.1), channel_id=1, source_target_pairs={{0,2},{1,3},{2,0},{3,1},{4,6},{5,7},{6,4},{7,5},{8,10},{9,11},{10,... | collective-permute-start | bytes 20152328 | tf_op jit(solution)/shard_map/ppermute | solution.py:33
  298.6 121.0 %copy-start.87 = (bf16[128,512]{1,0:T(8,128)(2,1)}, bf16[128,512]{1,0:T(8,128)(2,1)S(1)}, u32[]{:S(2)}) copy-start(bf16[128,512]{1,0:T(8,128)(2,1)S(1)} %get-tuple-element.2576) | copy-start | bytes 393220 | tf_op jit(solution)/shard_map/while
  301.9 68.2 %copy-start.244 = (f32[128]{0:T(128)}, f32[128]{0:T(128)S(1)}, u32[]{:S(2)}) copy-start(f32[128]{0:T(128)S(1)} %get-tuple-element.2274) | copy-start | bytes 1540 | tf_op jit(solution)/shard_map/while
  301.9 75.1 %copy-start.228 = (f32[128]{0:T(128)}, f32[128]{0:T(128)S(1)}, u32[]{:S(2)}) copy-start(f32[128]{0:T(128)S(1)} %get-tuple-element.2279) | copy-start | bytes 1540 | tf_op jit(solution)/shard_map/while
  301.9 117.8 %copy-start.200 = (f32[128]{0:T(128)}, f32[128]{0:T(128)S(1)}, u32[]{:S(2)}) copy-start(f32[128]{0:T(128)S(1)} %get-tuple-element.2289) | copy-start | bytes 1540 | tf_op jit(solution)/shard_map/while
  304.9 65.2 %copy-start.13 = (f32[32,32,128]{2,1,0:T(8,128)}, f32[32,32,128]{2,1,0:T(8,128)S(1)}, u32[]{:S(2)}) copy-start(f32[32,32,128]{2,1,0:T(8,128)S(1)} %fusion.787) | copy-start | bytes 1572868 | tf_op jit(solution)/shard_map/while
  322.2 227.1 %copy-start.24 = (f32[4,32,256]{2,1,0:T(8,128)}, f32[4,32,256]{2,1,0:T(8,128)S(1)}, u32[]{:S(2)}) copy-start(f32[4,32,256]{2,1,0:T(8,128)S(1)} %get-tuple-element.2261) | copy-start | bytes 393220 | tf_op jit(solution)/shard_map/while
  326.5 43.6 %copy-start.6 = (f32[4,32,32,128]{3,2,1,0:T(8,128)}, f32[4,32,32,128]{3,2,1,0:T(8,128)S(1)}, u32[]{:S(2)}) copy-start(f32[4,32,32,128]{3,2,1,0:T(8,128)S(1)} %get-tuple-element.2267) | copy-start | bytes 6291460 | tf_op jit(solution)/shard_map/while
  746.1 120.7 %copy-start.87 = (bf16[128,512]{1,0:T(8,128)(2,1)}, bf16[128,512]{1,0:T(8,128)(2,1)S(1)}, u32[]{:S(2)}) copy-start(bf16[128,512]{1,0:T(8,128)(2,1)S(1)} %get-tuple-element.2576) | copy-start | bytes 393220 | tf_op jit(solution)/shard_map/while
  749.3 67.9 %copy-start.244 = (f32[128]{0:T(128)}, f32[128]{0:T(128)S(1)}, u32[]{:S(2)}) copy-start(f32[128]{0:T(128)S(1)} %get-tuple-element.2274) | copy-start | bytes 1540 | tf_op jit(solution)/shard_map/while
  749.3 74.8 %copy-start.228 = (f32[128]{0:T(128)}, f32[128]{0:T(128)S(1)}, u32[]{:S(2)}) copy-start(f32[128]{0:T(128)S(1)} %get-tuple-element.2279) | copy-start | bytes 1540 | tf_op jit(solution)/shard_map/while
  749.3 117.5 %copy-start.200 = (f32[128]{0:T(128)}, f32[128]{0:T(128)S(1)}, u32[]{:S(2)}) copy-start(f32[128]{0:T(128)S(1)} %get-tuple-element.2289) | copy-start | bytes 1540 | tf_op jit(solution)/shard_map/while
  752.3 64.9 %copy-start.13 = (f32[32,32,128]{2,1,0:T(8,128)}, f32[32,32,128]{2,1,0:T(8,128)S(1)}, u32[]{:S(2)}) copy-start(f32[32,32,128]{2,1,0:T(8,128)S(1)} %fusion.787) | copy-start | bytes 1572868 | tf_op jit(solution)/shard_map/while
  769.7 227.5 %copy-start.24 = (f32[4,32,256]{2,1,0:T(8,128)}, f32[4,32,256]{2,1,0:T(8,128)S(1)}, u32[]{:S(2)}) copy-start(f32[4,32,256]{2,1,0:T(8,128)S(1)} %get-tuple-element.2261) | copy-start | bytes 393220 | tf_op jit(solution)/shard_map/while
  1197.0 121.1 %copy-start.87 = (bf16[128,512]{1,0:T(8,128)(2,1)}, bf16[128,512]{1,0:T(8,128)(2,1)S(1)}, u32[]{:S(2)}) copy-start(bf16[128,512]{1,0:T(8,128)(2,1)S(1)} %get-tuple-element.2576) | copy-start | bytes 393220 | tf_op jit(solution)/shard_map/while
  1200.2 67.9 %copy-start.244 = (f32[128]{0:T(128)}, f32[128]{0:T(128)S(1)}, u32[]{:S(2)}) copy-start(f32[128]{0:T(128)S(1)} %get-tuple-element.2274) | copy-start | bytes 1540 | tf_op jit(solution)/shard_map/while
  1200.2 74.9 %copy-start.228 = (f32[128]{0:T(128)}, f32[128]{0:T(128)S(1)}, u32[]{:S(2)}) copy-start(f32[128]{0:T(128)S(1)} %get-tuple-element.2279) | copy-start | bytes 1540 | tf_op jit(solution)/shard_map/while
  1200.2 117.8 %copy-start.200 = (f32[128]{0:T(128)}, f32[128]{0:T(128)S(1)}, u32[]{:S(2)}) copy-start(f32[128]{0:T(128)S(1)} %get-tuple-element.2289) | copy-start | bytes 1540 | tf_op jit(solution)/shard_map/while
  1203.3 64.9 %copy-start.13 = (f32[32,32,128]{2,1,0:T(8,128)}, f32[32,32,128]{2,1,0:T(8,128)S(1)}, u32[]{:S(2)}) copy-start(f32[32,32,128]{2,1,0:T(8,128)S(1)} %fusion.787) | copy-start | bytes 1572868 | tf_op jit(solution)/shard_map/while
  1220.6 227.7 %copy-start.24 = (f32[4,32,256]{2,1,0:T(8,128)}, f32[4,32,256]{2,1,0:T(8,128)S(1)}, u32[]{:S(2)}) copy-start(f32[4,32,256]{2,1,0:T(8,128)S(1)} %get-tuple-element.2261) | copy-start | bytes 393220 | tf_op jit(solution)/shard_map/while
  1648.1 121.0 %copy-start.87 = (bf16[128,512]{1,0:T(8,128)(2,1)}, bf16[128,512]{1,0:T(8,128)(2,1)S(1)}, u32[]{:S(2)}) copy-start(bf16[128,512]{1,0:T(8,128)(2,1)S(1)} %get-tuple-element.2576) | copy-start | bytes 393220 | tf_op jit(solution)/shard_map/while
  1651.3 68.2 %copy-start.244 = (f32[128]{0:T(128)}, f32[128]{0:T(128)S(1)}, u32[]{:S(2)}) copy-start(f32[128]{0:T(128)S(1)} %get-tuple-element.2274) | copy-start | bytes 1540 | tf_op jit(solution)/shard_map/while
  1651.3 75.1 %copy-start.228 = (f32[128]{0:T(128)}, f32[128]{0:T(128)S(1)}, u32[]{:S(2)}) copy-start(f32[128]{0:T(128)S(1)} %get-tuple-element.2279) | copy-start | bytes 1540 | tf_op jit(solution)/shard_map/while
  1651.3 117.7 %copy-start.200 = (f32[128]{0:T(128)}, f32[128]{0:T(128)S(1)}, u32[]{:S(2)}) copy-start(f32[128]{0:T(128)S(1)} %get-tuple-element.2289) | copy-start | bytes 1540 | tf_op jit(solution)/shard_map/while
  1654.4 65.2 %copy-start.13 = (f32[32,32,128]{2,1,0:T(8,128)}, f32[32,32,128]{2,1,0:T(8,128)S(1)}, u32[]{:S(2)}) copy-start(f32[32,32,128]{2,1,0:T(8,128)S(1)} %fusion.787) | copy-start | bytes 1572868 | tf_op jit(solution)/shard_map/while
  1671.7 227.8 %copy-start.24 = (f32[4,32,256]{2,1,0:T(8,128)}, f32[4,32,256]{2,1,0:T(8,128)S(1)}, u32[]{:S(2)}) copy-start(f32[4,32,256]{2,1,0:T(8,128)S(1)} %get-tuple-element.2261) | copy-start | bytes 393220 | tf_op jit(solution)/shard_map/while
  1676.0 43.6 %copy-start.6 = (f32[4,32,32,128]{3,2,1,0:T(8,128)}, f32[4,32,32,128]{3,2,1,0:T(8,128)S(1)}, u32[]{:S(2)}) copy-start(f32[4,32,32,128]{3,2,1,0:T(8,128)S(1)} %get-tuple-element.2267) | copy-start | bytes 6291460 | tf_op jit(solution)/shard_map/while
  2170.8 130.5 %copy-start.127 = (f32[3580,128]{1,0:T(8,128)S(1)}, f32[3580,128]{1,0:T(8,128)}, u32[]{:S(2)}) copy-start(f32[3580,128]{1,0:T(8,128)} %param.13) | copy-start | bytes 5498884
  (1039 other events, 4181.0 us)
Sparse Core Ops, SparseCore 0:
  10.1 48.7 all-gather.5
  60.5 82.3 all-gather.3
  2128.4 167.4 all-reduce.34
